TPU v7x, 32 devices: a whole 2x2x4 slice. The times are simulated.
32 devices in a mesh: src: 4 (over z), delay: 8 (over y, x, core).
Axes of the slice: x: 2, y: 2, z: 4, core: 2. Of those that a mesh axis runs over, the one named last changes fastest.
Arguments:
- history: float32 [32, 16, 16, 128], P('delay', 'src'), may hold values from -6 to 6
- slot_map: int32 [32], P('delay'), may hold values from 0 to 3, as said below
- interaction: float32 [1536, 128, 128], P(('src', 'delay')), may hold values from -0.0546875 to 0.0546875
- pattern: int32 [3, 1536], P(None, ('src', 'delay')), may hold values from 0 to 15, as said below
- live: int32 [32], P(('src', 'delay')), may hold values from 12 to 48
- near_inverse: float32 [16, 128, 128], P('src'), may hold values from -0.5 to 0.5
- incident: float32 [4, 16, 16, 128], P(None, 'src'), may hold values from -6 to 6
Outputs:
- currents: float32 [4, 16, 16, 128], P(None, 'src')
Inputs may be any that keep to these rules, and one draw needn't show every extreme that they name: `slot_map`: each band's 4 entries are a cyclic rotation of 0 .. 3. `pattern`: row 0 lies in 0 .. 3, row 1 in 0 .. 15, row 2 in 0 .. 3.
All inputs are finite; a program needn't handle non-finite values.
Results may differ from a plain program's by a relative error of at most 0.0003.
Values sent between devices are 32-bit elements; how exact they have to be, the bound alone decides.
No kernel may reach another device: no remote copies, remote signals or barrier semaphores. Data moves between devices by JAX's collectives and lax.ppermute only.
A program may use at most 64 MiB of HBM per device.

v0:
```python
import jax
import jax.numpy as jnp
from jax import lax
from jax.sharding import PartitionSpec as P


def shifted(x, axis, by):
    devices = lax.axis_size(axis)
    pairs = [(i, i + by) for i in range(devices) if 0 <= i + by < devices]
    return lax.ppermute(x, axis, pairs)


def slot_holding(slot_map, wanted, moment):
    length = slot_map.shape[0]
    positions = jnp.arange(length, dtype=jnp.int32)
    return jnp.sum(jnp.where((slot_map + moment) % length == wanted, positions, 0))


def body(history, slot_map, interaction, pattern, live, near_inverse, incident):
    slot_count = history.shape[0]
    group_blocks = history.shape[1]
    columns = history.shape[2]
    block_width = history.shape[3]
    moments = incident.shape[0]
    pair_count = interaction.shape[0]
    positions = jnp.arange(slot_count, dtype=jnp.int32)
    at_front = lax.axis_index("delay") == 0
    in_use = (jnp.arange(pair_count, dtype=jnp.int32) < live[0]).astype(jnp.float32)
    row_match = pattern[0][None, :] == jnp.arange(group_blocks, dtype=jnp.int32)[:, None]
    selector = row_match.astype(jnp.float32) * in_use[None, :]
    band_state = lax.all_gather(history, "src", axis=1, tiled=True)
    results = []
    newest = None
    for moment in range(moments):
        if moment > 0:
            vacated = slot_holding(slot_map, slot_count - 1, moment - 1)
            outgoing_slot = lax.dynamic_index_in_dim(band_state, vacated, 0, keepdims=False)
            incoming = shifted(outgoing_slot, "delay", 1)
            entering = jnp.where(at_front, newest, incoming)
            band_state = lax.dynamic_update_index_in_dim(band_state, entering, vacated, 0)
        holder_match = (slot_map[None, :] + moment) % slot_count == pattern[2][:, None]
        holder = jnp.sum(jnp.where(holder_match, positions[None, :], 0), axis=1)
        picked = band_state[holder, pattern[1]]
        products = jnp.einsum("pab,prb->pra", interaction, picked, precision=lax.Precision.HIGHEST)
        partial_field = jnp.dot(
            selector,
            products.reshape(pair_count, columns * block_width),
            precision=lax.Precision.HIGHEST,
        )
        partial_field = partial_field.reshape(group_blocks, columns, block_width)
        field_sum = lax.psum(partial_field, "delay")
        current = jnp.einsum(
            "iab,irb->ira",
            near_inverse,
            incident[moment] - field_sum,
            precision=lax.Precision.HIGHEST,
        )
        results.append(current)
        if moment + 1 < moments:
            newest = lax.all_gather(current, "src", axis=0, tiled=True)
    return jnp.stack(results)


def solution(mesh):
    return jax.shard_map(
        body,
        mesh=mesh,
        in_specs=(
            P("delay", "src", None, None),
            P("delay"),
            P(("src", "delay"), None, None),
            P(None, ("src", "delay")),
            P(("src", "delay")),
            P("src", None, None),
            P(None, "src", None, None),
        ),
        out_specs=P(None, "src", None, None),
        check_vma=False,
    )
```

profile of v0, /device:TPU:4, one launch (start us, length us, event | category | flops | bytes accessed | tf_op | source)
XLA Modules:
  0.0 216.7 jit_solution(3523601571943106550)
XLA Ops:
  0.0 1.5 fusion.45
  1.5 18.1 %all_gather.12 = f32[4,16,16,128]{3,2,1,0:T(8,128)} all-gather(f32[4,4,16,128]{3,2,1,0:T(8,128)} %param.7), channel_id=1, replica_groups=mesh['src'=4,'delay'=8] {'src'}, dimensions={1}, use_global_device_ids=true | all-gather | bytes 655360 | tf_op jit(solution)/shard_map/all_gather | solution.py:31
  21.5 1.6 dynamic-slice_bitcast_fusion.2
  23.1 1.9 collective-permute-start
  26.6 2.6 %gather_fusion = f32[48,16,128]{2,1,0:T(8,128)} fusion(f32[4,16,16,128]{3,2,1,0:T(8,128)} %all_gather.12, s32[48]{0:T(128)S(1)} %get-tuple-element.25), kind=kCustom, calls=%fused_computation | custom fusion | bytes 786816 | tf_op jit(solution)/shard_map/gather | solution.py:43
  29.9 6.0 %fusion.74 = f32[48,16,128]{2,1,0:T(8,128)S(1)} fusion(f32[48,16,128]{2,1,0:T(8,128)} %gather_fusion, f32[48,128,128]{2,1,0:T(8,128)S(1)} %copy-done), kind=kOutput, calls=%fused_computation.121 | convolution fusion | flops 150994944 | bytes 3932160 | tf_op jit(solution)/shard_map/pab,prb->pra/dot_general | solution.py:44
  36.3 24.8 %psum.28 = f32[4,16,128]{2,0,1:T(4,128)S(1)} all-reduce(f32[4,16,128]{2,0,1:T(4,128)S(1)} %fusion.9), channel_id=1, replica_groups=mesh['src'=4,'delay'=8] {'delay'}, use_global_device_ids=true, to_apply=%region_1.2 | all-reduce | flops 8192 | bytes 65536 | tf_op jit(solution)/shard_map/psum | solution.py:51
  61.1 1.4 fusion.73
  66.7 13.4 %all_gather.13 = f32[16,16,128]{2,1,0:T(8,128)S(1)} all-gather(f32[4,16,128]{2,1,0:T(8,128)S(1)} %fusion.21), channel_id=1, replica_groups=mesh['src'=4,'delay'=8] {'src'}, dimensions={0}, use_global_device_ids=true | all-gather | bytes 163840 | tf_op jit(solution)/shard_map/all_gather | solution.py:60
  80.0 1.6 bitcast_dynamic-update-slice_fusion.2
  81.6 2.6 %gather_fusion.1 = f32[48,16,128]{2,1,0:T(8,128)} fusion(f32[4,16,16,128]{3,2,1,0:T(8,128)} %bitcast_dynamic-update-slice_fusion.2, s32[48]{0:T(128)S(1)} %get-tuple-element.24), kind=kCustom, calls=%fused_computation.1 | custom fusion | bytes 786816 | tf_op jit(solution)/shard_map/gather | solution.py:43
  84.3 6.0 %fusion.75 = f32[48,16,128]{2,1,0:T(8,128)S(1)} fusion(f32[48,16,128]{2,1,0:T(8,128)} %gather_fusion.1, f32[48,128,128]{2,1,0:T(8,128)S(1)} %copy-done), kind=kOutput, calls=%fused_computation.122 | convolution fusion | flops 150994944 | bytes 3932160 | tf_op jit(solution)/shard_map/pab,prb->pra/dot_general | solution.py:44
  90.2 1.0 fusion.6
  91.3 22.9 %psum.29 = f32[4,16,128]{2,0,1:T(4,128)S(1)} all-reduce(f32[4,16,128]{2,0,1:T(4,128)} %fusion.6), channel_id=1, replica_groups=mesh['src'=4,'delay'=8] {'delay'}, use_global_device_ids=true, to_apply=%region_4.5 | all-reduce | flops 8192 | bytes 65536 | tf_op jit(solution)/shard_map/psum | solution.py:51
  115.1 1.9 collective-permute-start.1
  117.6 13.9 %all_gather.14 = f32[16,16,128]{2,1,0:T(8,128)S(1)} all-gather(f32[4,16,128]{2,1,0:T(8,128)S(1)} %fusion.19), channel_id=1, replica_groups=mesh['src'=4,'delay'=8] {'src'}, dimensions={0}, use_global_device_ids=true | all-gather | bytes 163840 | tf_op jit(solution)/shard_map/all_gather | solution.py:60
  132.1 2.6 %gather_fusion.2 = f32[48,16,128]{2,1,0:T(8,128)} fusion(f32[4,16,16,128]{3,2,1,0:T(8,128)} %bitcast_dynamic-update-slice_fusion.1, s32[48]{0:T(128)S(1)} %get-tuple-element.23), kind=kCustom, calls=%fused_computation.2 | custom fusion | bytes 786816 | tf_op jit(solution)/shard_map/gather | solution.py:43
  134.7 6.0 %fusion.76 = f32[48,16,128]{2,1,0:T(8,128)S(1)} fusion(f32[48,16,128]{2,1,0:T(8,128)} %gather_fusion.2, f32[48,128,128]{2,1,0:T(8,128)S(1)} %copy-done), kind=kOutput, calls=%fused_computation.123 | convolution fusion | flops 150994944 | bytes 3932160 | tf_op jit(solution)/shard_map/pab,prb->pra/dot_general | solution.py:44
  141.7 22.9 %psum.30 = f32[4,16,128]{2,0,1:T(4,128)S(1)} all-reduce(f32[4,16,128]{2,0,1:T(4,128)} %fusion.3), channel_id=1, replica_groups=mesh['src'=4,'delay'=8] {'delay'}, use_global_device_ids=true, to_apply=%region_7.8 | all-reduce | flops 8192 | bytes 65536 | tf_op jit(solution)/shard_map/psum | solution.py:51
  165.6 1.9 collective-permute-start.2
  168.0 13.5 %all_gather.15 = f32[16,16,128]{2,1,0:T(8,128)S(1)} all-gather(f32[4,16,128]{2,1,0:T(8,128)S(1)} %fusion.17), channel_id=1, replica_groups=mesh['src'=4,'delay'=8] {'src'}, dimensions={0}, use_global_device_ids=true | all-gather | bytes 163840 | tf_op jit(solution)/shard_map/all_gather | solution.py:60
  182.2 2.6 %gather_fusion.3 = f32[48,16,128]{2,1,0:T(8,128)} fusion(f32[4,16,16,128]{3,2,1,0:T(8,128)} %bitcast_dynamic-update-slice_fusion, s32[48]{0:T(128)S(1)} %get-tuple-element.9), kind=kCustom, calls=%fused_computation.3 | custom fusion | bytes 786816 | tf_op jit(solution)/shard_map/gather | solution.py:43
  184.9 6.0 %fusion.77 = f32[48,16,128]{2,1,0:T(8,128)S(1)} fusion(f32[48,16,128]{2,1,0:T(8,128)} %gather_fusion.3, f32[48,128,128]{2,1,0:T(8,128)S(1)} %copy-done), kind=kOutput, calls=%fused_computation.124 | convolution fusion | flops 150994944 | bytes 3932160 | tf_op jit(solution)/shard_map/pab,prb->pra/dot_general | solution.py:44
  191.9 22.9 %psum.31 = f32[4,16,128]{2,0,1:T(4,128)S(1)} all-reduce(f32[4,16,128]{2,0,1:T(4,128)} %fusion), channel_id=1, replica_groups=mesh['src'=4,'delay'=8] {'delay'}, use_global_device_ids=true, to_apply=%region_10.11 | all-reduce | flops 8192 | bytes 65536 | tf_op jit(solution)/shard_map/psum | solution.py:51
  (34 shorter events, 10.8 us)
Async XLA Ops:
  0.0 29.9 %copy-start = (f32[48,128,128]{2,1,0:T(8,128)S(1)}, f32[48,128,128]{2,1,0:T(8,128)}, u32[]{:S(2)}) copy-start(f32[48,128,128]{2,1,0:T(8,128)} %param.9) | copy-start | bytes 9437188
  1.5 61.0 %copy-start.1 = (f32[4,128,128]{2,1,0:T(8,128)S(1)}, f32[4,128,128]{2,1,0:T(8,128)}, u32[]{:S(2)}) copy-start(f32[4,128,128]{2,1,0:T(8,128)} %param.12) | copy-start | bytes 786436
  23.1 56.9 %collective-permute-start = (f32[16,16,128]{2,1,0:T(8,128)}, f32[16,16,128]{2,1,0:T(8,128)}, u32[]{:S(2)}, u32[]{:S(2)}) collective-permute-start(f32[16,16,128]{2,1,0:T(8,128)} %dynamic-slice_bitcast_fusion.2), channel_id=1, source_target_pairs={{0,1},{1,2},{2,3},{3,4},{4,5},{5,6},{6,7},{8,9},{9,10},{10,11},{11... | collective-permute-start | bytes 393224 | tf_op jit(solution)/shard_map/ppermute | solution.py:10
  29.9 6.0 %copy-start.2 = (f32[48]{0:T(128)}, f32[48]{0:T(128)S(1)}, u32[]{:S(2)}) copy-start(f32[48]{0:T(128)S(1)} %compare_convert_fusion) | copy-start | bytes 580
  62.5 27.7 %copy-start.3 = (f32[48]{0:T(128)S(1)}, f32[48]{0:T(128)}, u32[]{:S(2)}) copy-start(f32[48]{0:T(128)} %copy-done.2) | copy-start | bytes 580
  90.2 50.5 %copy-start.4 = (f32[48]{0:T(128)S(1)}, f32[48]{0:T(128)}, u32[]{:S(2)}) copy-start(f32[48]{0:T(128)} %copy-done.2) | copy-start | bytes 580
  115.1 16.3 %collective-permute-start.1 = (f32[16,16,128]{2,1,0:T(8,128)S(1)}, f32[16,16,128]{2,1,0:T(8,128)S(1)}, u32[]{:S(2)}, u32[]{:S(2)}) collective-permute-start(f32[16,16,128]{2,1,0:T(8,128)S(1)} %dynamic-slice_bitcast_fusion.1), channel_id=1, source_target_pairs={{0,1},{1,2},{2,3},{3,4},{4,5},{5,6},{6,7},{8,9},{9,10},{10,11},{11... | collective-permute-start | bytes 393224 | tf_op jit(solution)/shard_map/ppermute | solution.py:10
  165.6 16.0 %collective-permute-start.2 = (f32[16,16,128]{2,1,0:T(8,128)S(1)}, f32[16,16,128]{2,1,0:T(8,128)S(1)}, u32[]{:S(2)}, u32[]{:S(2)}) collective-permute-start(f32[16,16,128]{2,1,0:T(8,128)S(1)} %dynamic-slice_bitcast_fusion), channel_id=1, source_target_pairs={{0,1},{1,2},{2,3},{3,4},{4,5},{5,6},{6,7},{8,9},{9,10},{10,11},{11... | collective-permute-start | bytes 393224 | tf_op jit(solution)/shard_map/ppermute | solution.py:10
where the time goes:
time: 218 us; the launch traced here: 217 us
  blocking collectives  152 us (70%)
  matrix products  29.4 us (13%)
  local copies, waits for them, and re-layouts  16.2 us (7%)
  other arithmetic  6.73 us (3%)
  between operations  6.34 us (3%)
  starting transfers between devices  5.75 us (3%)
    psum x4, blocking collectives, body(): field_sum = lax.psum(partial_field, 'delay')  93.5 us
    all_gather x3, blocking collectives, body(): newest = lax.all_gather(current, 'src', axis=0, tiled=True)  40.7 us
    dot_general x4, matrix products, body(): jnp.einsum('pab,prb->pra', interaction, picked, precision=lax.Precision.H...  23.8 us
    all_gather x1, blocking collectives, body(): band_state = lax.all_gather(history, 'src', axis=1, tiled=True)  18.1 us
    gather x4, local copies, waits for them, and re-layouts, body(): picked = band_state[holder, pattern[1]]  10.6 us
    ppermute x3, starting transfers between devices, shifted(): return lax.ppermute(x, axis, pairs)  5.75 us
  transfers between devices with their start and end apart: 3, of which 0 were waited for; matrix products, arithmetic and copies ran while one was open for 6% of the time, Pallas kernels for 0%

commit v1 on v0

--- a/solution.py
+++ b/solution.py
@@ -2,6 +2,12 @@
 import jax.numpy as jnp
 from jax import lax
 from jax.sharding import PartitionSpec as P
+
+
+def gather_and_add(value, axis):
+    pieces = lax.all_gather(value, axis, axis=0, tiled=False)
+    total = pieces.sum(axis=0)
+    return total
 
 
 def shifted(x, axis, by):
@@ -48,7 +54,7 @@
             precision=lax.Precision.HIGHEST,
         )
         partial_field = partial_field.reshape(group_blocks, columns, block_width)
-        field_sum = lax.psum(partial_field, "delay")
+        field_sum = gather_and_add(partial_field, "delay")
         current = jnp.einsum(
             "iab,irb->ira",
             near_inverse,

time: 218 us -> 171 us (0.78); the launches traced: 217 us -> 167 us
  blocking collectives: 152 us -> 97.9 us
  other arithmetic: 6.73 us -> 12.7 us
    psum x4 -> x0, blocking collectives: 93.5 us -> none  [body(): field_sum = lax.psum(partial_field, 'delay')]
    all_gather x0 -> x4, blocking collectives: none -> 39.5 us  [gather_and_add(): pieces = lax.all_gather(value, axis, axis=0, tiled=False)]
    reduce_sum x0 -> x4, other arithmetic: none -> 3.89 us  [gather_and_add(): total = pieces.sum(axis=0)]
  transfers between devices with their start and end apart: 3 -> 3, of which waited for: 0 -> 0; matrix products, arithmetic and copies ran while one was open for 6% -> 9% of each run, Pallas kernels for 0% -> 0%
where the time goes in v1:
time: 171 us; the launch traced here: 167 us
  blocking collectives  97.9 us (57%)
  matrix products  27.5 us (16%)
  local copies, waits for them, and re-layouts  16 us (9%)
  other arithmetic  12.7 us (7%)
  starting transfers between devices  6.56 us (4%)
  between operations  6.51 us (4%)
    all_gather x3, blocking collectives, body(): newest = lax.all_gather(current, 'src', axis=0, tiled=True)  40.3 us
    all_gather x4, blocking collectives, gather_and_add(): pieces = lax.all_gather(value, axis, axis=0, tiled=False)  39.5 us
    dot_general x4, matrix products, body(): jnp.einsum('pab,prb->pra', interaction, picked, precision=lax.Precision.H...  23.8 us
    all_gather x1, blocking collectives, body(): band_state = lax.all_gather(history, 'src', axis=1, tiled=True)  18.1 us
    gather x4, local copies, waits for them, and re-layouts, body(): picked = band_state[holder, pattern[1]]  10.6 us
    ppermute x3, starting transfers between devices, shifted(): return lax.ppermute(x, axis, pairs)  6.56 us
    reduce_sum x4, other arithmetic, gather_and_add(): total = pieces.sum(axis=0)  3.89 us
  transfers between devices with their start and end apart: 3, of which 0 were waited for; matrix products, arithmetic and copies ran while one was open for 9% of the time, Pallas kernels for 0%

profile of v1, /device:TPU:4, one launch (start us, length us, event | category | flops | bytes accessed | tf_op | source)
XLA Modules:
  0.0 167.2 jit_solution(2118773219303339827)
XLA Ops:
  0.0 2.1 %fusion.45 = (s32[]{:T(128)}, s32[4]{0:T(128)S(1)}, s32[]{:T(128)}, s32[4]{0:T(128)S(1)}, s32[]{:T(128)}, /*index=5*/s32[4]{0:T(128)}, s32[4]{0:T(128)}) fusion(s32[4]{0:T(128)} %param.8), kind=kLoop, calls=%fused_computation.91 | loop fusion | flops 221 | bytes 92 | tf_op jit(solution)/shard_map/reduce_sum | solution.py:22
  2.1 18.1 %all_gather.24 = f32[4,16,16,128]{3,2,1,0:T(8,128)} all-gather(f32[4,4,16,128]{3,2,1,0:T(8,128)} %param.7), channel_id=1, replica_groups=mesh['src'=4,'delay'=8] {'src'}, dimensions={1}, use_global_device_ids=true | all-gather | bytes 655360 | tf_op jit(solution)/shard_map/all_gather | solution.py:37
  22.1 1.6 dynamic-slice_bitcast_fusion.2
  23.7 2.0 %collective-permute-start = (f32[16,16,128]{2,1,0:T(8,128)}, f32[16,16,128]{2,1,0:T(8,128)}, u32[]{:S(2)}, u32[]{:S(2)}) collective-permute-start(f32[16,16,128]{2,1,0:T(8,128)} %dynamic-slice_bitcast_fusion.2), channel_id=1, source_target_pairs={{0,1},{1,2},{2,3},{3,4},{4,5},{5,6},{6,7},{8,9},{9,10},{10,11},{11... | collective-permute-start | bytes 393224 | tf_op jit(solution)/shard_map/ppermute | solution.py:16
  25.7 1.3 slice_bitcast_fusion.1
  28.5 2.6 %gather_fusion = f32[48,16,128]{2,1,0:T(8,128)} fusion(f32[4,16,16,128]{3,2,1,0:T(8,128)} %all_gather.24, s32[48]{0:T(128)S(1)} %get-tuple-element.25), kind=kCustom, calls=%fused_computation | custom fusion | bytes 786816 | tf_op jit(solution)/shard_map/gather | solution.py:49
  31.8 6.0 %fusion.74 = f32[48,16,128]{2,1,0:T(8,128)S(1)} fusion(f32[48,16,128]{2,1,0:T(8,128)} %gather_fusion, f32[48,128,128]{2,1,0:T(8,128)S(1)} %copy-done), kind=kOutput, calls=%fused_computation.121 | convolution fusion | flops 150994944 | bytes 3932160 | tf_op jit(solution)/shard_map/pab,prb->pra/dot_general | solution.py:50
  38.2 10.4 %all-gather = f32[32,16,128]{2,1,0:T(8,128)} all-gather(f32[4,16,128]{2,1,0:T(8,128)S(1)} %copy.34), channel_id=2, replica_groups=mesh['src'=4,'delay'=8] {'delay'}, dimensions={0}, use_global_device_ids=true | all-gather | bytes 294912 | tf_op jit(solution)/shard_map/all_gather | solution.py:8
  49.3 1.0 reduce_sum.109
  55.3 13.3 %all_gather.26 = f32[16,16,128]{2,1,0:T(8,128)S(1)} all-gather(f32[4,16,128]{2,1,0:T(8,128)S(1)} %fusion.21), channel_id=1, replica_groups=mesh['src'=4,'delay'=8] {'src'}, dimensions={0}, use_global_device_ids=true | all-gather | bytes 163840 | tf_op jit(solution)/shard_map/all_gather | solution.py:66
  68.7 1.6 bitcast_dynamic-update-slice_fusion.2
  70.3 2.6 %gather_fusion.1 = f32[48,16,128]{2,1,0:T(8,128)} fusion(f32[4,16,16,128]{3,2,1,0:T(8,128)} %bitcast_dynamic-update-slice_fusion.2, s32[48]{0:T(128)S(1)} %get-tuple-element.24), kind=kCustom, calls=%fused_computation.1 | custom fusion | bytes 786816 | tf_op jit(solution)/shard_map/gather | solution.py:49
  72.9 6.0 %fusion.75 = f32[48,16,128]{2,1,0:T(8,128)S(1)} fusion(f32[48,16,128]{2,1,0:T(8,128)} %gather_fusion.1, f32[48,128,128]{2,1,0:T(8,128)S(1)} %copy-done), kind=kOutput, calls=%fused_computation.122 | convolution fusion | flops 150994944 | bytes 3932160 | tf_op jit(solution)/shard_map/pab,prb->pra/dot_general | solution.py:50
  79.3 9.4 %all-gather.1 = f32[32,16,128]{2,1,0:T(8,128)} all-gather(f32[4,16,128]{2,1,0:T(8,128)S(1)} %copy.39), channel_id=3, replica_groups=mesh['src'=4,'delay'=8] {'delay'}, dimensions={0}, use_global_device_ids=true | all-gather | bytes 294912 | tf_op jit(solution)/shard_map/all_gather | solution.py:8
  90.6 2.3 %collective-permute-start.1 = (f32[16,16,128]{2,1,0:T(8,128)S(1)}, f32[16,16,128]{2,1,0:T(8,128)S(1)}, u32[]{:S(2)}, u32[]{:S(2)}) collective-permute-start(f32[16,16,128]{2,1,0:T(8,128)S(1)} %dynamic-slice_bitcast_fusion.1), channel_id=1, source_target_pairs={{0,1},{1,2},{2,3},{3,4},{4,5},{5,6},{6,7},{8,9},{9,10},{10,11},{11... | collective-permute-start | bytes 393224 | tf_op jit(solution)/shard_map/ppermute | solution.py:16
  93.4 13.6 %all_gather.28 = f32[16,16,128]{2,1,0:T(8,128)S(1)} all-gather(f32[4,16,128]{2,1,0:T(8,128)S(1)} %fusion.19), channel_id=1, replica_groups=mesh['src'=4,'delay'=8] {'src'}, dimensions={0}, use_global_device_ids=true | all-gather | bytes 163840 | tf_op jit(solution)/shard_map/all_gather | solution.py:66
  107.7 2.6 %gather_fusion.2 = f32[48,16,128]{2,1,0:T(8,128)} fusion(f32[4,16,16,128]{3,2,1,0:T(8,128)} %bitcast_dynamic-update-slice_fusion.1, s32[48]{0:T(128)S(1)} %get-tuple-element.23), kind=kCustom, calls=%fused_computation.2 | custom fusion | bytes 786816 | tf_op jit(solution)/shard_map/gather | solution.py:49
  110.3 6.0 %fusion.76 = f32[48,16,128]{2,1,0:T(8,128)S(1)} fusion(f32[48,16,128]{2,1,0:T(8,128)} %gather_fusion.2, f32[48,128,128]{2,1,0:T(8,128)S(1)} %copy-done), kind=kOutput, calls=%fused_computation.123 | convolution fusion | flops 150994944 | bytes 3932160 | tf_op jit(solution)/shard_map/pab,prb->pra/dot_general | solution.py:50
  116.7 10.2 %all-gather.2 = f32[32,16,128]{2,1,0:T(8,128)} all-gather(f32[4,16,128]{2,1,0:T(8,128)S(1)} %copy.44), channel_id=4, replica_groups=mesh['src'=4,'delay'=8] {'delay'}, dimensions={0}, use_global_device_ids=true | all-gather | bytes 294912 | tf_op jit(solution)/shard_map/all_gather | solution.py:8
  128.8 2.3 %collective-permute-start.2 = (f32[16,16,128]{2,1,0:T(8,128)S(1)}, f32[16,16,128]{2,1,0:T(8,128)S(1)}, u32[]{:S(2)}, u32[]{:S(2)}) collective-permute-start(f32[16,16,128]{2,1,0:T(8,128)S(1)} %dynamic-slice_bitcast_fusion), channel_id=1, source_target_pairs={{0,1},{1,2},{2,3},{3,4},{4,5},{5,6},{6,7},{8,9},{9,10},{10,11},{11... | collective-permute-start | bytes 393224 | tf_op jit(solution)/shard_map/ppermute | solution.py:16
  131.6 13.4 %all_gather.30 = f32[16,16,128]{2,1,0:T(8,128)S(1)} all-gather(f32[4,16,128]{2,1,0:T(8,128)S(1)} %fusion.17), channel_id=1, replica_groups=mesh['src'=4,'delay'=8] {'src'}, dimensions={0}, use_global_device_ids=true | all-gather | bytes 163840 | tf_op jit(solution)/shard_map/all_gather | solution.py:66
  145.7 2.6 %gather_fusion.3 = f32[48,16,128]{2,1,0:T(8,128)} fusion(f32[4,16,16,128]{3,2,1,0:T(8,128)} %bitcast_dynamic-update-slice_fusion, s32[48]{0:T(128)S(1)} %get-tuple-element.9), kind=kCustom, calls=%fused_computation.3 | custom fusion | bytes 786816 | tf_op jit(solution)/shard_map/gather | solution.py:49
  148.3 6.0 %fusion.77 = f32[48,16,128]{2,1,0:T(8,128)S(1)} fusion(f32[48,16,128]{2,1,0:T(8,128)} %gather_fusion.3, f32[48,128,128]{2,1,0:T(8,128)S(1)} %copy-done), kind=kOutput, calls=%fused_computation.124 | convolution fusion | flops 150994944 | bytes 3932160 | tf_op jit(solution)/shard_map/pab,prb->pra/dot_general | solution.py:50
  154.7 9.5 %all-gather.3 = f32[32,16,128]{2,1,0:T(8,128)} all-gather(f32[4,16,128]{2,1,0:T(8,128)S(1)} %copy.49), channel_id=5, replica_groups=mesh['src'=4,'delay'=8] {'delay'}, dimensions={0}, use_global_device_ids=true | all-gather | bytes 294912 | tf_op jit(solution)/shard_map/all_gather | solution.py:8
  (52 shorter events, 14.3 us)
Async XLA Ops:
  0.0 31.8 %copy-start = (f32[48,128,128]{2,1,0:T(8,128)S(1)}, f32[48,128,128]{2,1,0:T(8,128)}, u32[]{:S(2)}) copy-start(f32[48,128,128]{2,1,0:T(8,128)} %param.9) | copy-start | bytes 9437188
  2.1 46.6 %copy-start.2 = (f32[4,4,16,128]{3,2,1,0:T(8,128)S(1)}, f32[4,4,16,128]{3,2,1,0:T(8,128)}, u32[]{:S(2)}) copy-start(f32[4,4,16,128]{3,2,1,0:T(8,128)} %param.13) | copy-start | bytes 393220
  23.7 27.4 %copy-start.1 = (f32[4,128,128]{2,1,0:T(8,128)S(1)}, f32[4,128,128]{2,1,0:T(8,128)}, u32[]{:S(2)}) copy-start(f32[4,128,128]{2,1,0:T(8,128)} %param.12) | copy-start | bytes 786436
  23.7 45.0 %collective-permute-start = (f32[16,16,128]{2,1,0:T(8,128)}, f32[16,16,128]{2,1,0:T(8,128)}, u32[]{:S(2)}, u32[]{:S(2)}) collective-permute-start(f32[16,16,128]{2,1,0:T(8,128)} %dynamic-slice_bitcast_fusion.2), channel_id=1, source_target_pairs={{0,1},{1,2},{2,3},{3,4},{4,5},{5,6},{6,7},{8,9},{9,10},{10,11},{11... | collective-permute-start | bytes 393224 | tf_op jit(solution)/shard_map/ppermute | solution.py:16
  31.1 6.6 %copy-start.5 = (s32[48]{0:T(128)S(1)}, s32[48]{0:T(128)}, u32[]{:S(2)}) copy-start(s32[48]{0:T(128)} %get-tuple-element.21) | copy-start | bytes 580
  31.8 17.5 %copy-start.7 = (f32[48]{0:T(128)}, f32[48]{0:T(128)S(1)}, u32[]{:S(2)}) copy-start(f32[48]{0:T(128)S(1)} %compare_convert_fusion) | copy-start | bytes 580
  49.3 29.6 %copy-start.6 = (s32[48]{0:T(128)S(1)}, s32[48]{0:T(128)}, u32[]{:S(2)}) copy-start(s32[48]{0:T(128)} %get-tuple-element.21) | copy-start | bytes 580
  49.3 29.6 %copy-start.8 = (f32[48]{0:T(128)S(1)}, f32[48]{0:T(128)}, u32[]{:S(2)}) copy-start(f32[48]{0:T(128)} %copy-done.7) | copy-start | bytes 580
  70.3 22.6 %copy-start.4 = (f32[1,4,16,128]{3,2,1,0:T(8,128)S(1)}, f32[1,4,16,128]{3,2,1,0:T(8,128)}, u32[]{:S(2)}) copy-start(f32[1,4,16,128]{3,2,1,0:T(8,128)} %get-tuple-element.18) | copy-start | bytes 98308
  88.7 27.6 %copy-start.9 = (f32[48]{0:T(128)S(1)}, f32[48]{0:T(128)}, u32[]{:S(2)}) copy-start(f32[48]{0:T(128)} %copy-done.7) | copy-start | bytes 580
  90.6 16.4 %collective-permute-start.1 = (f32[16,16,128]{2,1,0:T(8,128)S(1)}, f32[16,16,128]{2,1,0:T(8,128)S(1)}, u32[]{:S(2)}, u32[]{:S(2)}) collective-permute-start(f32[16,16,128]{2,1,0:T(8,128)S(1)} %dynamic-slice_bitcast_fusion.1), channel_id=1, source_target_pairs={{0,1},{1,2},{2,3},{3,4},{4,5},{5,6},{6,7},{8,9},{9,10},{10,11},{11... | collective-permute-start | bytes 393224 | tf_op jit(solution)/shard_map/ppermute | solution.py:16
  107.7 23.4 %copy-start.3 = (f32[1,4,16,128]{3,2,1,0:T(8,128)S(1)}, f32[1,4,16,128]{3,2,1,0:T(8,128)}, u32[]{:S(2)}) copy-start(f32[1,4,16,128]{3,2,1,0:T(8,128)} %get-tuple-element.17) | copy-start | bytes 98308
  128.8 16.2 %collective-permute-start.2 = (f32[16,16,128]{2,1,0:T(8,128)S(1)}, f32[16,16,128]{2,1,0:T(8,128)S(1)}, u32[]{:S(2)}, u32[]{:S(2)}) collective-permute-start(f32[16,16,128]{2,1,0:T(8,128)S(1)} %dynamic-slice_bitcast_fusion), channel_id=1, source_target_pairs={{0,1},{1,2},{2,3},{3,4},{4,5},{5,6},{6,7},{8,9},{9,10},{10,11},{11... | collective-permute-start | bytes 393224 | tf_op jit(solution)/shard_map/ppermute | solution.py:16
